TPU v7x, 32 devices: a whole 2x2x4 slice. The times are simulated.
32 devices in a mesh: uly: 8 (over z, y), blk: 4 (over x, core).
Axes of the slice: x: 2, y: 2, z: 4, core: 2. Of those that a mesh axis runs over, the one named last changes fastest.
Arguments:
- queries: bfloat16 [2048, 2048], P(('blk', 'uly')), may hold values from -20 to 20
- keys: bfloat16 [2048, 2048], P(('blk', 'uly')), may hold values from -20 to 20
- values: bfloat16 [2048, 2048], P(('blk', 'uly')), may hold values from -6 to 6
- block_list: int32 [32, 16, 16], P('uly', 'blk'), may hold values from -1 to 15, as said below
Outputs:
- attended: bfloat16 [2048, 2048], P(('blk', 'uly'))
Inputs may be any that keep to these rules, and one draw needn't show every extreme that they name: block_list[h, b, 0] = b; every other entry is -1 (an empty slot) or a block below b, and the blocks named in one list are distinct.
All inputs are finite; a program needn't handle non-finite values.
Results may differ from a plain program's by a relative error of at most 0.0045.
Values may be sent and summed in bfloat16 or wider, within the bound.
No kernel may reach another device: no remote copies, remote signals or barrier semaphores. Data moves between devices by JAX's collectives and lax.ppermute only.
A program may use at most 64 MiB of HBM per device.

v0:
```python
import jax
import jax.numpy as jnp
from jax import lax
from jax.sharding import PartitionSpec as P

BLOCK = 128
QGROUP = 2


def head_major(token_rows, heads_local, head_dim):
    return token_rows.reshape(token_rows.shape[0] // BLOCK, BLOCK, heads_local, head_dim).transpose(
        2, 0, 1, 3
    )


def select_blocks(source, chosen):
    return jnp.take(source, chosen, axis=0)


def attend_block(operand):
    query_group, key_slots, value_slots, chosen, query_block = operand
    scale = query_group.shape[-1] ** (-0.5)
    scores = (
        jnp.einsum("abd,asjd->absj", query_group, key_slots, preferred_element_type=jnp.float32)
        * scale
    )
    positions = jnp.arange(BLOCK, dtype=jnp.int32)
    query_pos = query_block[:, None] * BLOCK + positions[None, :]
    key_pos = jnp.maximum(chosen, 0)[:, :, None] * BLOCK + positions[None, None, :]
    allowed = (chosen[:, None, :, None] >= 0) & (
        key_pos[:, None, :, :] <= query_pos[:, :, None, None]
    )
    scores = jnp.where(allowed, scores, -1e30)
    row_max = jnp.max(scores, axis=(2, 3), keepdims=True)
    weights = jnp.where(allowed, jnp.exp(scores - row_max), 0.0)
    denominator = jnp.sum(weights, axis=(2, 3))
    rounded = weights.astype(jnp.bfloat16)
    summed = jnp.einsum("absj,asjd->abd", rounded, value_slots, preferred_element_type=jnp.float32)
    return (summed / denominator[:, :, None]).astype(jnp.bfloat16)


def local(queries, keys, values, block_list):
    heads_local = block_list.shape[0]
    blocks_dev = block_list.shape[1]
    slot_count = block_list.shape[2]
    head_dim = queries.shape[1] // (heads_local * lax.axis_size("uly"))
    first_block = lax.axis_index("blk") * blocks_dev
    query_rows, key_rows, value_rows = (
        lax.all_to_all(queries, "uly", split_axis=1, concat_axis=0, tiled=True),
        lax.all_to_all(keys, "uly", split_axis=1, concat_axis=0, tiled=True),
        lax.all_to_all(values, "uly", split_axis=1, concat_axis=0, tiled=True),
    )
    keys_all = lax.all_gather(key_rows, "blk", axis=0, tiled=True)
    values_all = lax.all_gather(value_rows, "blk", axis=0, tiled=True)
    chosen = jnp.maximum(block_list, 0)
    key_slots = jax.vmap(select_blocks)(head_major(keys_all, heads_local, head_dim), chosen)
    value_slots = jax.vmap(select_blocks)(head_major(values_all, heads_local, head_dim), chosen)
    key_slots, value_slots = (key_slots, value_slots)
    groups = heads_local * blocks_dev // QGROUP
    query_heads = head_major(query_rows, heads_local, head_dim).reshape(
        groups, QGROUP, BLOCK, head_dim
    )
    key_groups = key_slots.reshape(groups, QGROUP, slot_count, BLOCK, head_dim)
    value_groups = value_slots.reshape(groups, QGROUP, slot_count, BLOCK, head_dim)
    list_groups = block_list.reshape(groups, QGROUP, slot_count)
    block_numbers = first_block + jnp.arange(blocks_dev, dtype=jnp.int32)
    block_groups = jnp.broadcast_to(block_numbers[None, :], (heads_local, blocks_dev)).reshape(
        groups, QGROUP
    )
    result = lax.map(
        attend_block, (query_heads, key_groups, value_groups, list_groups, block_groups)
    )
    result = result.reshape(heads_local, blocks_dev * BLOCK, head_dim).transpose(1, 0, 2)
    result = result.reshape(blocks_dev * BLOCK, heads_local * head_dim)
    return lax.all_to_all(result, "uly", split_axis=0, concat_axis=1, tiled=True)


def solution(mesh):
    placed = (
        P(("blk", "uly"), None),
        P(("blk", "uly"), None),
        P(("blk", "uly"), None),
        P("uly", "blk", None),
    )
    return jax.shard_map(
        local, mesh=mesh, in_specs=placed, out_specs=P(("blk", "uly"), None), check_vma=False
    )
```

profile of v0, /device:TPU:0, one launch (start us, length us, event | category | flops | bytes accessed | tf_op | source)
XLA Modules:
  0.0 148.7 jit_solution(14057702400680355051)
XLA Ops:
  7.6 16.1 %all_to_all.73 = bf16[64,8,256]{2,0,1:T(8,128)(2,1)} all-to-all(bf16[64,8,256]{2,0,1:T(8,128)(2,1)S(1)} %bitcast.102), channel_id=1, replica_groups=mesh['uly'=8,'blk'=4] {'uly'}, dimensions={1} | all-to-all | bytes 524288 | tf_op jit(solution)/shard_map/all_to_all | solution.py:50
  24.7 12.1 %all_to_all.74 = bf16[64,8,256]{2,0,1:T(8,128)(2,1)} all-to-all(bf16[64,8,256]{2,0,1:T(8,128)(2,1)S(1)} %bitcast.103), channel_id=1, replica_groups=mesh['uly'=8,'blk'=4] {'uly'}, dimensions={1} | all-to-all | bytes 524288 | tf_op jit(solution)/shard_map/all_to_all | solution.py:51
  37.5 3.6 %all-to-all-start = ((bf16[64,8,256]{2,0,1:T(8,128)(2,1)}), bf16[64,8,256]{2,0,1:T(8,128)(2,1)S(1)}, u32[]{:S(2)}, u32[]{:S(2)}) async-start(bf16[64,8,256]{2,0,1:T(8,128)(2,1)} %bitcast.73), calls=%async_computation | async-start | bytes 524288 | tf_op jit(solution)/shard_map/all_to_all | solution.py:49
  41.3 8.3 %all-to-all-done = bf16[64,8,256]{2,0,1:T(8,128)(2,1)S(1)} async-done(((bf16[64,8,256]{2,0,1:T(8,128)(2,1)}), bf16[64,8,256]{2,0,1:T(8,128)(2,1)S(1)}, u32[]{:S(2)}, u32[]{:S(2)}) %all-to-all-start) | async-done | bytes 262176 | tf_op jit(solution)/shard_map/all_to_all | solution.py:49
  50.3 3.3 %reshape.151 = bf16[16,128,4,64]{3,2,1,0:T(4,128)(2,1)S(1)} reshape(bf16[2048,256]{1,0:T(8,128)(2,1)} %all-gather.3.cloned.1.call-done) | data formatting | bytes 2097152 | tf_op jit(solution)/shard_map/reshape | solution.py:11
  55.0 2.8 %all-gather.5.cloned.1.call-done = bf16[2048,256]{1,0:T(8,128)(2,1)} async-done(((bf16[512,256]{1,0:T(8,128)(2,1)}), bf16[2048,256]{1,0:T(8,128)(2,1)}) %all-gather.5.cloned.1.call-update) | async-done | bytes 1048592 | tf_op jit(solution)/shard_map/all_gather | solution.py:54
  57.9 4.4 %reshape.152 = bf16[16,128,4,64]{3,2,1,0:T(4,128)(2,1)} reshape(bf16[2048,256]{1,0:T(8,128)(2,1)} %all-gather.5.cloned.1.call-done) | data formatting | bytes 2097152 | tf_op jit(solution)/shard_map/reshape | solution.py:11
  62.3 3.0 %copy.52 = bf16[16,128,4,64]{1,3,0,2:T(8,128)(2,1)S(1)} copy(bf16[16,128,4,64]{3,2,1,0:T(4,128)(2,1)} %reshape.152) | data formatting | bytes 2097152 | tf_op jit(solution)/shard_map/reshape | solution.py:11
  65.3 3.3 %gather_fusion = bf16[256,128,64]{1,2,0:T(8,128)(2,1)} fusion(bf16[4,16,128,64]{2,3,1,0:T(8,128)(2,1)S(1)} %bitcast.90, s32[256]{0:T(256)S(1)} %reshape.139), kind=kCustom, calls=%fused_computation.clone | custom fusion | bytes 8390656 | tf_op jit(solution)/shard_map/vmap(jit(_take))/gather | solution.py:17
  68.6 3.3 %gather_fusion.1 = bf16[256,128,64]{1,2,0:T(8,128)(2,1)} fusion(bf16[4,16,128,64]{2,3,1,0:T(8,128)(2,1)S(1)} %bitcast.91, s32[256]{0:T(256)S(1)} %reshape.139), kind=kCustom, calls=%fused_computation.1.clone | custom fusion | bytes 8390656 | tf_op jit(solution)/shard_map/vmap(jit(_take))/gather | solution.py:17
  72.0 5.9 %broadcast_select_fusion = (bf16[4,4,16,128,64]{3,4,2,1,0:T(8,128)(2,1)}, bf16[4,4,16,128,64]{3,4,2,1,0:T(8,128)(2,1)}) fusion(bf16[4,4,16,128,64]{3,4,2,1,0:T(8,128)(2,1)} %bitcast.93, pred[4,4,16]{2,1,0:T(4,128)(4,1)S(1)} %maximum_compare_fusion, bf16[4,4,16,128,64]{3,4,2,1,0:T(8,128)(2,1)} %bitcast.92), kind=kLoop, calls=%fused_computation.33 | loop fusion | flops 4194304 | bytes 16777472 | tf_op jit(solution)/shard_map/vmap(jit(_take))/select_n | solution.py:17
  77.9 47.7 %while.10 = (s32[]{:T(128)}, bf16[8,2,128,64]{2,1,0,3:T(2,128)(2,1)S(1)}, s32[8,2,16]{2,1,0:T(2,128)S(1)}, s32[8,2]{1,0:T(8,128)S(1)}, bf16[8,2,128,64]{2,3,1,0:...) while((s32[]{:T(128)}, ...), condition=%wide.region_3.5_spmd, body=%wide.region_0.4_spmd.sunk | while | flops 142118752 | bytes 7548637 | solution.py:70
  78.1 2.9 %fusion.31 = (f32[2,128]{1,0:T(2,128)S(1)}, f32[2,128,16,128]{1,3,2,0:T(8,128)S(1)}) fusion(bf16[8,2,16,128,64]{3,4,2,1,0:T(8,128)(2,1)} %get-tuple-element.165, s32[]{:T(128)} %get-tuple-element.152, bf16[8,2,128,64]{2,3,1,0:T(8,128)(2,1)S(1)} %get-tuple-element.164, s32[2,128]{1,0:T(2,128)S(1)} %iota_add_fusion.4, ...), kind=kOutput, calls=%fused_computation.41.clone.1 | convolution fusion | flops 69730048 | bytes 2674176 | tf_op jit(solution)/shard_map/while/body/eval_jaxpr/abd,asjd->absj/dot_general | solution.py:24
  81.8 2.1 %fusion.33 = bf16[1,2,128,64]{2,3,1,0:T(8,128)(2,1)S(1)} fusion(f32[2,128,16,128]{1,3,2,0:T(8,128)S(1)} %get-tuple-element.142, f32[2,128]{1,0:T(2,128)S(1)} %get-tuple-element.143, s32[2,128]{1,0:T(2,128)S(1)} %iota_add_fusion.4, s32[2,16,128]{2,1,0:T(8,128)S(1)} %iota_add_fusion.5, pred[2,16]{1,0:T(4,128)(4,1)S(1)} %compare_bitcast_fusion.2, ...), kind=kOutput, calls=%fused_computation.10.clone.1 | convolution fusion | flops 69763072 | bytes 2674208 | tf_op jit(solution)/shard_map/while/body/eval_jaxpr/absj,asjd->abd/dot_general | solution.py:38
  84.1 2.9 %fusion.31 = (f32[2,128]{1,0:T(2,128)S(1)}, f32[2,128,16,128]{1,3,2,0:T(8,128)S(1)}) fusion(bf16[8,2,16,128,64]{3,4,2,1,0:T(8,128)(2,1)} %get-tuple-element.165, s32[]{:T(128)} %get-tuple-element.152, bf16[8,2,128,64]{2,3,1,0:T(8,128)(2,1)S(1)} %get-tuple-element.164, s32[2,128]{1,0:T(2,128)S(1)} %iota_add_fusion.4, ...), kind=kOutput, calls=%fused_computation.41.clone.1 | convolution fusion | flops 69730048 | bytes 2674176 | tf_op jit(solution)/shard_map/while/body/eval_jaxpr/abd,asjd->absj/dot_general | solution.py:24
  90.1 2.9 %fusion.31 = (f32[2,128]{1,0:T(2,128)S(1)}, f32[2,128,16,128]{1,3,2,0:T(8,128)S(1)}) fusion(bf16[8,2,16,128,64]{3,4,2,1,0:T(8,128)(2,1)} %get-tuple-element.165, s32[]{:T(128)} %get-tuple-element.152, bf16[8,2,128,64]{2,3,1,0:T(8,128)(2,1)S(1)} %get-tuple-element.164, s32[2,128]{1,0:T(2,128)S(1)} %iota_add_fusion.4, ...), kind=kOutput, calls=%fused_computation.41.clone.1 | convolution fusion | flops 69730048 | bytes 2674176 | tf_op jit(solution)/shard_map/while/body/eval_jaxpr/abd,asjd->absj/dot_general | solution.py:24
  96.0 2.9 %fusion.31 = (f32[2,128]{1,0:T(2,128)S(1)}, f32[2,128,16,128]{1,3,2,0:T(8,128)S(1)}) fusion(bf16[8,2,16,128,64]{3,4,2,1,0:T(8,128)(2,1)} %get-tuple-element.165, s32[]{:T(128)} %get-tuple-element.152, bf16[8,2,128,64]{2,3,1,0:T(8,128)(2,1)S(1)} %get-tuple-element.164, s32[2,128]{1,0:T(2,128)S(1)} %iota_add_fusion.4, ...), kind=kOutput, calls=%fused_computation.41.clone.1 | convolution fusion | flops 69730048 | bytes 2674176 | tf_op jit(solution)/shard_map/while/body/eval_jaxpr/abd,asjd->absj/dot_general | solution.py:24
  99.7 2.1 %fusion.33 = bf16[1,2,128,64]{2,3,1,0:T(8,128)(2,1)S(1)} fusion(f32[2,128,16,128]{1,3,2,0:T(8,128)S(1)} %get-tuple-element.142, f32[2,128]{1,0:T(2,128)S(1)} %get-tuple-element.143, s32[2,128]{1,0:T(2,128)S(1)} %iota_add_fusion.4, s32[2,16,128]{2,1,0:T(8,128)S(1)} %iota_add_fusion.5, pred[2,16]{1,0:T(4,128)(4,1)S(1)} %compare_bitcast_fusion.2, ...), kind=kOutput, calls=%fused_computation.10.clone.1 | convolution fusion | flops 69763072 | bytes 2674208 | tf_op jit(solution)/shard_map/while/body/eval_jaxpr/absj,asjd->abd/dot_general | solution.py:38
  102.0 2.9 %fusion.31 = (f32[2,128]{1,0:T(2,128)S(1)}, f32[2,128,16,128]{1,3,2,0:T(8,128)S(1)}) fusion(bf16[8,2,16,128,64]{3,4,2,1,0:T(8,128)(2,1)} %get-tuple-element.165, s32[]{:T(128)} %get-tuple-element.152, bf16[8,2,128,64]{2,3,1,0:T(8,128)(2,1)S(1)} %get-tuple-element.164, s32[2,128]{1,0:T(2,128)S(1)} %iota_add_fusion.4, ...), kind=kOutput, calls=%fused_computation.41.clone.1 | convolution fusion | flops 69730048 | bytes 2674176 | tf_op jit(solution)/shard_map/while/body/eval_jaxpr/abd,asjd->absj/dot_general | solution.py:24
  108.0 2.9 %fusion.31 = (f32[2,128]{1,0:T(2,128)S(1)}, f32[2,128,16,128]{1,3,2,0:T(8,128)S(1)}) fusion(bf16[8,2,16,128,64]{3,4,2,1,0:T(8,128)(2,1)} %get-tuple-element.165, s32[]{:T(128)} %get-tuple-element.152, bf16[8,2,128,64]{2,3,1,0:T(8,128)(2,1)S(1)} %get-tuple-element.164, s32[2,128]{1,0:T(2,128)S(1)} %iota_add_fusion.4, ...), kind=kOutput, calls=%fused_computation.41.clone.1 | convolution fusion | flops 69730048 | bytes 2674176 | tf_op jit(solution)/shard_map/while/body/eval_jaxpr/abd,asjd->absj/dot_general | solution.py:24
  113.9 2.9 %fusion.31 = (f32[2,128]{1,0:T(2,128)S(1)}, f32[2,128,16,128]{1,3,2,0:T(8,128)S(1)}) fusion(bf16[8,2,16,128,64]{3,4,2,1,0:T(8,128)(2,1)} %get-tuple-element.165, s32[]{:T(128)} %get-tuple-element.152, bf16[8,2,128,64]{2,3,1,0:T(8,128)(2,1)S(1)} %get-tuple-element.164, s32[2,128]{1,0:T(2,128)S(1)} %iota_add_fusion.4, ...), kind=kOutput, calls=%fused_computation.41.clone.1 | convolution fusion | flops 69730048 | bytes 2674176 | tf_op jit(solution)/shard_map/while/body/eval_jaxpr/abd,asjd->absj/dot_general | solution.py:24
  117.6 2.1 %fusion.33 = bf16[1,2,128,64]{2,3,1,0:T(8,128)(2,1)S(1)} fusion(f32[2,128,16,128]{1,3,2,0:T(8,128)S(1)} %get-tuple-element.142, f32[2,128]{1,0:T(2,128)S(1)} %get-tuple-element.143, s32[2,128]{1,0:T(2,128)S(1)} %iota_add_fusion.4, s32[2,16,128]{2,1,0:T(8,128)S(1)} %iota_add_fusion.5, pred[2,16]{1,0:T(4,128)(4,1)S(1)} %compare_bitcast_fusion.2, ...), kind=kOutput, calls=%fused_computation.10.clone.1 | convolution fusion | flops 69763072 | bytes 2674208 | tf_op jit(solution)/shard_map/while/body/eval_jaxpr/absj,asjd->abd/dot_general | solution.py:38
  119.9 2.9 %fusion.31 = (f32[2,128]{1,0:T(2,128)S(1)}, f32[2,128,16,128]{1,3,2,0:T(8,128)S(1)}) fusion(bf16[8,2,16,128,64]{3,4,2,1,0:T(8,128)(2,1)} %get-tuple-element.165, s32[]{:T(128)} %get-tuple-element.152, bf16[8,2,128,64]{2,3,1,0:T(8,128)(2,1)S(1)} %get-tuple-element.164, s32[2,128]{1,0:T(2,128)S(1)} %iota_add_fusion.4, ...), kind=kOutput, calls=%fused_computation.41.clone.1 | convolution fusion | flops 69730048 | bytes 2674176 | tf_op jit(solution)/shard_map/while/body/eval_jaxpr/abd,asjd->absj/dot_general | solution.py:24
  126.5 14.6 %all_to_all.75 = bf16[8,64,256]{2,1,0:T(8,128)(2,1)S(1)} all-to-all(bf16[8,64,256]{2,1,0:T(8,128)(2,1)S(1)} %reshape.153), channel_id=1, replica_groups=mesh['uly'=8,'blk'=4] {'uly'}, dimensions={0} | all-to-all | bytes 524288 | tf_op jit(solution)/shard_map/all_to_all | solution.py:75
  (89 shorter events, 24.8 us)
Async XLA Ops:
  6.5 30.3 %copy-start = (bf16[64,2048]{1,0:T(8,128)(2,1)S(1)}, bf16[64,2048]{1,0:T(8,128)(2,1)}, u32[]{:S(2)}) copy-start(bf16[64,2048]{1,0:T(8,128)(2,1)} %param.8) | copy-start | bytes 786436
  6.5 34.6 %copy-start.2 = (s32[4,4,16]{2,1,0:T(4,128)S(1)}, s32[4,4,16]{2,1,0:T(4,128)}, u32[]{:S(2)}) copy-start(s32[4,4,16]{2,1,0:T(4,128)} %param.11) | copy-start | bytes 3076
  6.5 43.7 %all-gather.3.cloned.1.call-start = ((), (), s32[]{:S(2)}) async-start(), calls=%async_computation.4 | async-start | bytes 1310720 | tf_op jit(solution)/shard_map/all_gather | solution.py:53
  23.7 34.1 %all-gather.5.cloned.1.call-start = ((), (), s32[]{:S(2)}) async-start(), calls=%async_computation.5 | async-start | bytes 1310720 | tf_op jit(solution)/shard_map/all_gather | solution.py:54
  37.5 12.1 %all-to-all-start = ((bf16[64,8,256]{2,0,1:T(8,128)(2,1)}), bf16[64,8,256]{2,0,1:T(8,128)(2,1)S(1)}, u32[]{:S(2)}, u32[]{:S(2)}) async-start(bf16[64,8,256]{2,0,1:T(8,128)(2,1)} %bitcast.73), calls=%async_computation | async-start | bytes 524288 | tf_op jit(solution)/shard_map/all_to_all | solution.py:49
  72.0 6.0 %copy-start.1 = (bf16[8,2,128,64]{2,1,0,3:T(2,128)(2,1)S(1)}, bf16[8,2,128,64]{2,1,0,3:T(2,128)(2,1)}, u32[]{:S(2)}) copy-start(bf16[8,2,128,64]{2,1,0,3:T(2,128)(2,1)} %custom-call.6) | copy-start | bytes 786436
Sparse Core Ops, SparseCore 0:
  23.8 15.6 all-gather.2
  41.1 16.6 all-gather.4
where the time goes:
time: 150 us; the launch traced here: 149 us
  blocking collectives  42.8 us (29%)
  matrix products  39.3 us (26%)
  local copies, waits for them, and re-layouts  24.3 us (16%)
  other arithmetic  13.5 us (9%)
  between operations  13.5 us (9%)
  waiting for transfers between devices  11.2 us (7%)
  starting transfers between devices  3.63 us (2%)
    dot_general x8, matrix products, attend_block(): jnp.einsum('abd,asjd->absj', query_group, key_slots, preferred_element_ty...  22.8 us
    dot_general x8, matrix products, attend_block(): jnp.einsum('absj,asjd->abd', rounded, value_slots, preferred_element_type...  16.4 us
    all_to_all x1, blocking collectives, local(): lax.all_to_all(keys, 'uly', split_axis=1, concat_axis=0, tiled=True)  16.1 us
    all_to_all x1, blocking collectives, local(): lax.all_to_all(result, 'uly', split_axis=0, concat_axis=1, tiled=True)  14.6 us
    reshape x5, local copies, waits for them, and re-layouts, head_major(): token_rows.reshape(token_rows.shape[0] // BLOCK, BLOCK, heads_local, head...  12.4 us
    all_to_all x1, blocking collectives, local(): lax.all_to_all(values, 'uly', split_axis=1, concat_axis=0, tiled=True)  12.1 us
    all_to_all x1, waiting for transfers between devices, local(): lax.all_to_all(queries, 'uly', split_axis=1, concat_axis=0, tiled=True)  8.31 us
    gather x3, local copies, waits for them, and re-layouts, select_blocks(): return jnp.take(source, chosen, axis=0)  6.75 us
  transfers between devices with their start and end apart: 3, of which 2 were waited for; matrix products, arithmetic and copies ran while one was open for 5% of the time, Pallas kernels for 0%

commit v1 on v0

--- a/solution.py
+++ b/solution.py
@@ -5,6 +5,22 @@
 
 BLOCK = 128
 QGROUP = 2
+
+
+def exchange_in_pairs(value, axis, split, join):
+    ways, here = (lax.axis_size(axis), lax.axis_index(axis))
+    width = value.shape[split] // ways
+    shape = list(value.shape)
+    shape[split] = width
+    height = shape[join]
+    shape[join] = height * ways
+    full = jnp.zeros(shape, value.dtype)
+    for mask in range(ways):
+        part = lax.dynamic_slice_in_dim(value, (here ^ mask) * width, width, axis=split)
+        if mask:
+            part = lax.ppermute(part, axis, [(d, d ^ mask) for d in range(ways)])
+        full = lax.dynamic_update_slice_in_dim(full, part, (here ^ mask) * height, axis=join)
+    return full
 
 
 def head_major(token_rows, heads_local, head_dim):
@@ -46,7 +62,7 @@
     head_dim = queries.shape[1] // (heads_local * lax.axis_size("uly"))
     first_block = lax.axis_index("blk") * blocks_dev
     query_rows, key_rows, value_rows = (
-        lax.all_to_all(queries, "uly", split_axis=1, concat_axis=0, tiled=True),
+        exchange_in_pairs(queries, "uly", 1, 0),
         lax.all_to_all(keys, "uly", split_axis=1, concat_axis=0, tiled=True),
         lax.all_to_all(values, "uly", split_axis=1, concat_axis=0, tiled=True),
     )

time: 150 us -> 150 us (level)
  waiting for transfers between devices: 11.2 us -> 0.13 us
  starting transfers between devices: 3.63 us -> 11.3 us
  local copies, waits for them, and re-layouts: 24.3 us -> 28.4 us
    ppermute x0 -> x7, starting transfers between devices: none -> 11.3 us  [exchange_in_pairs(): part = lax.ppermute(part, axis, [(d, d ^ mask) for d in range(ways)])]
    all_to_all x1 -> x0, waiting for transfers between devices: 8.31 us -> none  [local(): lax.all_to_all(queries, 'uly', split_axis=1, concat_axis=0, tiled=True)]
    all_to_all x1 -> x0, starting transfers between devices: 3.59 us -> none  [local(): lax.all_to_all(queries, 'uly', split_axis=1, concat_axis=0, tiled=True)]
    dynamic_update_slice x0 -> x8, local copies, waits for them, and re-layouts: none -> 3.55 us  [exchange_in_pairs(): lax.dynamic_update_slice_in_dim(full, part, (here ^ mask) * height, axis=...]
    all_gather x1, waiting for transfers between devices: 2.84 us -> 0.02 us  [local(): values_all = lax.all_gather(value_rows, 'blk', axis=0, tiled=True)]
  transfers between devices with their start and end apart: 3 -> 9, of which waited for: 2 -> 1; matrix products, arithmetic and copies ran while one was open for 5% -> 8% of each run, Pallas kernels for 0% -> 0%
where the time goes in v1:
time: 150 us; the launch traced here: 149 us
  blocking collectives  41.9 us (28%)
  matrix products  39.5 us (26%)
  local copies, waits for them, and re-layouts  28.4 us (19%)
  between operations  13.7 us (9%)
  other arithmetic  13.5 us (9%)
  starting transfers between devices  11.3 us (8%)
    dot_general x8, matrix products, attend_block(): jnp.einsum('abd,asjd->absj', query_group, key_slots, preferred_element_ty...  23 us
    dot_general x8, matrix products, attend_block(): jnp.einsum('absj,asjd->abd', rounded, value_slots, preferred_element_type...  16.4 us
    all_to_all x1, blocking collectives, local(): lax.all_to_all(keys, 'uly', split_axis=1, concat_axis=0, tiled=True)  16.1 us
    all_to_all x1, blocking collectives, local(): lax.all_to_all(result, 'uly', split_axis=0, concat_axis=1, tiled=True)  13.8 us
    reshape x5, local copies, waits for them, and re-layouts, head_major(): token_rows.reshape(token_rows.shape[0] // BLOCK, BLOCK, heads_local, head...  12.3 us
    all_to_all x1, blocking collectives, local(): lax.all_to_all(values, 'uly', split_axis=1, concat_axis=0, tiled=True)  12.1 us
    ppermute x7, starting transfers between devices, exchange_in_pairs(): part = lax.ppermute(part, axis, [(d, d ^ mask) for d in range(ways)])  11.3 us
    gather x3, local copies, waits for them, and re-layouts, select_blocks(): return jnp.take(source, chosen, axis=0)  6.75 us
  transfers between devices with their start and end apart: 9, of which 1 were waited for; matrix products, arithmetic and copies ran while one was open for 8% of the time, Pallas kernels for 0%

profile of v1, /device:TPU:0, one launch (start us, length us, event | category | flops | bytes accessed | tf_op | source)
XLA Modules:
  0.0 148.9 jit_solution(1581803181235399956)
XLA Ops:
  7.6 16.1 %all_to_all.57 = bf16[64,8,256]{2,0,1:T(8,128)(2,1)} all-to-all(bf16[64,8,256]{2,0,1:T(8,128)(2,1)S(1)} %bitcast.97), channel_id=1, replica_groups=mesh['uly'=8,'blk'=4] {'uly'}, dimensions={1} | all-to-all | bytes 524288 | tf_op jit(solution)/shard_map/all_to_all | solution.py:66
  24.7 12.1 %all_to_all.58 = bf16[64,8,256]{2,0,1:T(8,128)(2,1)} all-to-all(bf16[64,8,256]{2,0,1:T(8,128)(2,1)S(1)} %bitcast.98), channel_id=1, replica_groups=mesh['uly'=8,'blk'=4] {'uly'}, dimensions={1} | all-to-all | bytes 524288 | tf_op jit(solution)/shard_map/all_to_all | solution.py:67
  41.5 2.8 %collective-permute-start.4 = (bf16[64,256]{1,0:T(8,128)(2,1)S(1)}, bf16[64,256]{1,0:T(8,128)(2,1)S(1)}, u32[]{:S(2)}, u32[]{:S(2)}) collective-permute-start(bf16[64,256]{1,0:T(8,128)(2,1)S(1)} %get-tuple-element.89), channel_id=1, source_target_pairs={{0,20},{4,16},{8,28},{12,24},{16,4},{20,0},{24,12},{28,8},{1,21},{... | collective-permute-start | bytes 98312 | tf_op jit(solution)/shard_map/ppermute | solution.py:21
  45.8 2.4 %collective-permute-start.6 = (bf16[64,256]{1,0:T(8,128)(2,1)S(1)}, bf16[64,256]{1,0:T(8,128)(2,1)S(1)}, u32[]{:S(2)}, u32[]{:S(2)}) collective-permute-start(bf16[64,256]{1,0:T(8,128)(2,1)S(1)} %get-tuple-element.88), channel_id=1, source_target_pairs={{0,28},{4,24},{8,20},{12,16},{16,12},{20,8},{24,4},{28,0},{1,29},{... | collective-permute-start | bytes 98312 | tf_op jit(solution)/shard_map/ppermute | solution.py:21
  53.9 3.3 %reshape.146 = bf16[16,128,4,64]{3,2,1,0:T(4,128)(2,1)S(1)} reshape(bf16[2048,256]{1,0:T(8,128)(2,1)} %all-gather.3.cloned.1.call-done) | data formatting | bytes 2097152 | tf_op jit(solution)/shard_map/reshape | solution.py:27
  58.7 4.4 %reshape.147 = bf16[16,128,4,64]{3,2,1,0:T(4,128)(2,1)} reshape(bf16[2048,256]{1,0:T(8,128)(2,1)} %all-gather.5.cloned.1.call-done) | data formatting | bytes 2097152 | tf_op jit(solution)/shard_map/reshape | solution.py:27
  63.1 3.0 %copy.58 = bf16[16,128,4,64]{1,3,0,2:T(8,128)(2,1)S(1)} copy(bf16[16,128,4,64]{3,2,1,0:T(4,128)(2,1)} %reshape.147) | data formatting | bytes 2097152 | tf_op jit(solution)/shard_map/reshape | solution.py:27
  66.2 3.3 %gather_fusion = bf16[256,128,64]{1,2,0:T(8,128)(2,1)} fusion(bf16[4,16,128,64]{2,3,1,0:T(8,128)(2,1)S(1)} %bitcast.86, s32[256]{0:T(256)S(1)} %reshape.135), kind=kCustom, calls=%fused_computation.clone | custom fusion | bytes 8390656 | tf_op jit(solution)/shard_map/vmap(jit(_take))/gather | solution.py:33
  69.5 3.4 %gather_fusion.1 = bf16[256,128,64]{1,2,0:T(8,128)(2,1)} fusion(bf16[4,16,128,64]{2,3,1,0:T(8,128)(2,1)S(1)} %bitcast.87, s32[256]{0:T(256)S(1)} %reshape.135), kind=kCustom, calls=%fused_computation.1.clone | custom fusion | bytes 8390656 | tf_op jit(solution)/shard_map/vmap(jit(_take))/gather | solution.py:33
  72.9 5.9 %broadcast_select_fusion = (bf16[4,4,16,128,64]{3,4,2,1,0:T(8,128)(2,1)}, bf16[4,4,16,128,64]{3,4,2,1,0:T(8,128)(2,1)}) fusion(bf16[4,4,16,128,64]{3,4,2,1,0:T(8,128)(2,1)} %bitcast.89, pred[4,4,16]{2,1,0:T(4,128)(4,1)S(1)} %maximum_compare_fusion, bf16[4,4,16,128,64]{3,4,2,1,0:T(8,128)(2,1)} %bitcast.88), kind=kLoop, calls=%fused_computation.33 | loop fusion | flops 4194304 | bytes 16777472 | tf_op jit(solution)/shard_map/vmap(jit(_take))/select_n | solution.py:33
  78.8 47.9 %while.10 = (s32[]{:T(128)}, bf16[8,2,128,64]{2,1,0,3:T(2,128)(2,1)S(1)}, s32[8,2,16]{2,1,0:T(2,128)S(1)}, s32[8,2]{1,0:T(8,128)S(1)}, bf16[8,2,128,64]{2,3,1,0:...) while((s32[]{:T(128)}, ...), condition=%wide.region_3.5_spmd, body=%wide.region_0.4_spmd.sunk | while | flops 142118752 | bytes 7548157 | solution.py:86
  78.9 2.9 %fusion.31 = (f32[2,128]{1,0:T(2,128)S(1)}, f32[2,128,16,128]{1,3,2,0:T(8,128)S(1)}) fusion(bf16[8,2,16,128,64]{3,4,2,1,0:T(8,128)(2,1)} %get-tuple-element.166, s32[]{:T(128)} %get-tuple-element.153, bf16[8,2,128,64]{2,3,1,0:T(8,128)(2,1)} %get-tuple-element.165, s32[2,128]{1,0:T(2,128)S(1)} %iota_add_fusion.4, ...), kind=kOutput, calls=%fused_computation.48.clone.1 | convolution fusion | flops 69730048 | bytes 2673696 | tf_op jit(solution)/shard_map/while/body/eval_jaxpr/abd,asjd->absj/dot_general | solution.py:40
  84.9 2.9 %fusion.31 = (f32[2,128]{1,0:T(2,128)S(1)}, f32[2,128,16,128]{1,3,2,0:T(8,128)S(1)}) fusion(bf16[8,2,16,128,64]{3,4,2,1,0:T(8,128)(2,1)} %get-tuple-element.166, s32[]{:T(128)} %get-tuple-element.153, bf16[8,2,128,64]{2,3,1,0:T(8,128)(2,1)} %get-tuple-element.165, s32[2,128]{1,0:T(2,128)S(1)} %iota_add_fusion.4, ...), kind=kOutput, calls=%fused_computation.48.clone.1 | convolution fusion | flops 69730048 | bytes 2673696 | tf_op jit(solution)/shard_map/while/body/eval_jaxpr/abd,asjd->absj/dot_general | solution.py:40
  88.6 2.1 %fusion.33 = bf16[1,2,128,64]{2,3,1,0:T(8,128)(2,1)S(1)} fusion(f32[2,128,16,128]{1,3,2,0:T(8,128)S(1)} %get-tuple-element.143, f32[2,128]{1,0:T(2,128)S(1)} %get-tuple-element.144, s32[2,128]{1,0:T(2,128)S(1)} %iota_add_fusion.4, s32[2,16,128]{2,1,0:T(8,128)S(1)} %iota_add_fusion.5, pred[2,16]{1,0:T(4,128)(4,1)S(1)} %compare_bitcast_fusion.2, ...), kind=kOutput, calls=%fused_computation.10.clone.1 | convolution fusion | flops 69763072 | bytes 2674208 | tf_op jit(solution)/shard_map/while/body/eval_jaxpr/absj,asjd->abd/dot_general | solution.py:54
  90.9 2.9 %fusion.31 = (f32[2,128]{1,0:T(2,128)S(1)}, f32[2,128,16,128]{1,3,2,0:T(8,128)S(1)}) fusion(bf16[8,2,16,128,64]{3,4,2,1,0:T(8,128)(2,1)} %get-tuple-element.166, s32[]{:T(128)} %get-tuple-element.153, bf16[8,2,128,64]{2,3,1,0:T(8,128)(2,1)} %get-tuple-element.165, s32[2,128]{1,0:T(2,128)S(1)} %iota_add_fusion.4, ...), kind=kOutput, calls=%fused_computation.48.clone.1 | convolution fusion | flops 69730048 | bytes 2673696 | tf_op jit(solution)/shard_map/while/body/eval_jaxpr/abd,asjd->absj/dot_general | solution.py:40
  94.6 2.1 %fusion.33 = bf16[1,2,128,64]{2,3,1,0:T(8,128)(2,1)S(1)} fusion(f32[2,128,16,128]{1,3,2,0:T(8,128)S(1)} %get-tuple-element.143, f32[2,128]{1,0:T(2,128)S(1)} %get-tuple-element.144, s32[2,128]{1,0:T(2,128)S(1)} %iota_add_fusion.4, s32[2,16,128]{2,1,0:T(8,128)S(1)} %iota_add_fusion.5, pred[2,16]{1,0:T(4,128)(4,1)S(1)} %compare_bitcast_fusion.2, ...), kind=kOutput, calls=%fused_computation.10.clone.1 | convolution fusion | flops 69763072 | bytes 2674208 | tf_op jit(solution)/shard_map/while/body/eval_jaxpr/absj,asjd->abd/dot_general | solution.py:54
  96.9 2.9 %fusion.31 = (f32[2,128]{1,0:T(2,128)S(1)}, f32[2,128,16,128]{1,3,2,0:T(8,128)S(1)}) fusion(bf16[8,2,16,128,64]{3,4,2,1,0:T(8,128)(2,1)} %get-tuple-element.166, s32[]{:T(128)} %get-tuple-element.153, bf16[8,2,128,64]{2,3,1,0:T(8,128)(2,1)} %get-tuple-element.165, s32[2,128]{1,0:T(2,128)S(1)} %iota_add_fusion.4, ...), kind=kOutput, calls=%fused_computation.48.clone.1 | convolution fusion | flops 69730048 | bytes 2673696 | tf_op jit(solution)/shard_map/while/body/eval_jaxpr/abd,asjd->absj/dot_general | solution.py:40
  100.6 2.1 %fusion.33 = bf16[1,2,128,64]{2,3,1,0:T(8,128)(2,1)S(1)} fusion(f32[2,128,16,128]{1,3,2,0:T(8,128)S(1)} %get-tuple-element.143, f32[2,128]{1,0:T(2,128)S(1)} %get-tuple-element.144, s32[2,128]{1,0:T(2,128)S(1)} %iota_add_fusion.4, s32[2,16,128]{2,1,0:T(8,128)S(1)} %iota_add_fusion.5, pred[2,16]{1,0:T(4,128)(4,1)S(1)} %compare_bitcast_fusion.2, ...), kind=kOutput, calls=%fused_computation.10.clone.1 | convolution fusion | flops 69763072 | bytes 2674208 | tf_op jit(solution)/shard_map/while/body/eval_jaxpr/absj,asjd->abd/dot_general | solution.py:54
  102.9 2.9 %fusion.31 = (f32[2,128]{1,0:T(2,128)S(1)}, f32[2,128,16,128]{1,3,2,0:T(8,128)S(1)}) fusion(bf16[8,2,16,128,64]{3,4,2,1,0:T(8,128)(2,1)} %get-tuple-element.166, s32[]{:T(128)} %get-tuple-element.153, bf16[8,2,128,64]{2,3,1,0:T(8,128)(2,1)} %get-tuple-element.165, s32[2,128]{1,0:T(2,128)S(1)} %iota_add_fusion.4, ...), kind=kOutput, calls=%fused_computation.48.clone.1 | convolution fusion | flops 69730048 | bytes 2673696 | tf_op jit(solution)/shard_map/while/body/eval_jaxpr/abd,asjd->absj/dot_general | solution.py:40
  106.6 2.1 %fusion.33 = bf16[1,2,128,64]{2,3,1,0:T(8,128)(2,1)S(1)} fusion(f32[2,128,16,128]{1,3,2,0:T(8,128)S(1)} %get-tuple-element.143, f32[2,128]{1,0:T(2,128)S(1)} %get-tuple-element.144, s32[2,128]{1,0:T(2,128)S(1)} %iota_add_fusion.4, s32[2,16,128]{2,1,0:T(8,128)S(1)} %iota_add_fusion.5, pred[2,16]{1,0:T(4,128)(4,1)S(1)} %compare_bitcast_fusion.2, ...), kind=kOutput, calls=%fused_computation.10.clone.1 | convolution fusion | flops 69763072 | bytes 2674208 | tf_op jit(solution)/shard_map/while/body/eval_jaxpr/absj,asjd->abd/dot_general | solution.py:54
  108.9 2.9 %fusion.31 = (f32[2,128]{1,0:T(2,128)S(1)}, f32[2,128,16,128]{1,3,2,0:T(8,128)S(1)}) fusion(bf16[8,2,16,128,64]{3,4,2,1,0:T(8,128)(2,1)} %get-tuple-element.166, s32[]{:T(128)} %get-tuple-element.153, bf16[8,2,128,64]{2,3,1,0:T(8,128)(2,1)} %get-tuple-element.165, s32[2,128]{1,0:T(2,128)S(1)} %iota_add_fusion.4, ...), kind=kOutput, calls=%fused_computation.48.clone.1 | convolution fusion | flops 69730048 | bytes 2673696 | tf_op jit(solution)/shard_map/while/body/eval_jaxpr/abd,asjd->absj/dot_general | solution.py:40
  114.9 2.9 %fusion.31 = (f32[2,128]{1,0:T(2,128)S(1)}, f32[2,128,16,128]{1,3,2,0:T(8,128)S(1)}) fusion(bf16[8,2,16,128,64]{3,4,2,1,0:T(8,128)(2,1)} %get-tuple-element.166, s32[]{:T(128)} %get-tuple-element.153, bf16[8,2,128,64]{2,3,1,0:T(8,128)(2,1)} %get-tuple-element.165, s32[2,128]{1,0:T(2,128)S(1)} %iota_add_fusion.4, ...), kind=kOutput, calls=%fused_computation.48.clone.1 | convolution fusion | flops 69730048 | bytes 2673696 | tf_op jit(solution)/shard_map/while/body/eval_jaxpr/abd,asjd->absj/dot_general | solution.py:40
  120.9 2.9 %fusion.31 = (f32[2,128]{1,0:T(2,128)S(1)}, f32[2,128,16,128]{1,3,2,0:T(8,128)S(1)}) fusion(bf16[8,2,16,128,64]{3,4,2,1,0:T(8,128)(2,1)} %get-tuple-element.166, s32[]{:T(128)} %get-tuple-element.153, bf16[8,2,128,64]{2,3,1,0:T(8,128)(2,1)} %get-tuple-element.165, s32[2,128]{1,0:T(2,128)S(1)} %iota_add_fusion.4, ...), kind=kOutput, calls=%fused_computation.48.clone.1 | convolution fusion | flops 69730048 | bytes 2673696 | tf_op jit(solution)/shard_map/while/body/eval_jaxpr/abd,asjd->absj/dot_general | solution.py:40
  127.5 13.8 %all_to_all.59 = bf16[8,64,256]{2,1,0:T(8,128)(2,1)S(1)} all-to-all(bf16[8,64,256]{2,1,0:T(8,128)(2,1)S(1)} %reshape.148), channel_id=1, replica_groups=mesh['uly'=8,'blk'=4] {'uly'}, dimensions={0} | all-to-all | bytes 524288 | tf_op jit(solution)/shard_map/all_to_all | solution.py:91
  (116 shorter events, 33.0 us)
Async XLA Ops:
  6.5 30.3 %copy-start = (bf16[64,2048]{1,0:T(8,128)(2,1)S(1)}, bf16[64,2048]{1,0:T(8,128)(2,1)}, u32[]{:S(2)}) copy-start(bf16[64,2048]{1,0:T(8,128)(2,1)} %param.8) | copy-start | bytes 786436
  6.5 37.8 %copy-start.1 = (s32[4,4,16]{2,1,0:T(4,128)S(1)}, s32[4,4,16]{2,1,0:T(4,128)}, u32[]{:S(2)}) copy-start(s32[4,4,16]{2,1,0:T(4,128)} %param.11) | copy-start | bytes 3076
  6.5 47.4 %all-gather.3.cloned.1.call-start = ((), (), s32[]{:S(2)}) async-start(), calls=%async_computation.3 | async-start | bytes 1310720 | tf_op jit(solution)/shard_map/all_gather | solution.py:69
  23.7 35.0 %all-gather.5.cloned.1.call-start = ((), (), s32[]{:S(2)}) async-start(), calls=%async_computation.4 | async-start | bytes 1310720 | tf_op jit(solution)/shard_map/all_gather | solution.py:70
  36.9 7.4 %collective-permute-start = (bf16[64,256]{1,0:T(8,128)(2,1)S(1)}, bf16[64,256]{1,0:T(8,128)(2,1)S(1)}, u32[]{:S(2)}, u32[]{:S(2)}) collective-permute-start(bf16[64,256]{1,0:T(8,128)(2,1)S(1)} %get-tuple-element.93), channel_id=1, source_target_pairs={{0,4},{4,0},{8,12},{12,8},{16,20},{20,16},{24,28},{28,24},{1,5},{5... | collective-permute-start | bytes 98312 | tf_op jit(solution)/shard_map/ppermute | solution.py:21
  38.5 7.4 %collective-permute-start.1 = (bf16[64,256]{1,0:T(8,128)(2,1)S(1)}, bf16[64,256]{1,0:T(8,128)(2,1)S(1)}, u32[]{:S(2)}, u32[]{:S(2)}) collective-permute-start(bf16[64,256]{1,0:T(8,128)(2,1)S(1)} %get-tuple-element.92), channel_id=1, source_target_pairs={{0,8},{4,12},{8,0},{12,4},{16,24},{20,28},{24,16},{28,20},{1,9},{5... | collective-permute-start | bytes 98312 | tf_op jit(solution)/shard_map/ppermute | solution.py:21
  38.5 11.6 %collective-permute-start.2 = (bf16[64,256]{1,0:T(8,128)(2,1)S(1)}, bf16[64,256]{1,0:T(8,128)(2,1)S(1)}, u32[]{:S(2)}, u32[]{:S(2)}) collective-permute-start(bf16[64,256]{1,0:T(8,128)(2,1)S(1)} %get-tuple-element.91), channel_id=1, source_target_pairs={{0,12},{4,8},{8,4},{12,0},{16,28},{20,24},{24,20},{28,16},{1,13},{... | collective-permute-start | bytes 98312 | tf_op jit(solution)/shard_map/ppermute | solution.py:21
  40.5 10.3 %collective-permute-start.3 = (bf16[64,256]{1,0:T(8,128)(2,1)S(1)}, bf16[64,256]{1,0:T(8,128)(2,1)S(1)}, u32[]{:S(2)}, u32[]{:S(2)}) collective-permute-start(bf16[64,256]{1,0:T(8,128)(2,1)S(1)} %get-tuple-element.90), channel_id=1, source_target_pairs={{0,16},{4,20},{8,24},{12,28},{16,0},{20,4},{24,8},{28,12},{1,17},{... | collective-permute-start | bytes 98312 | tf_op jit(solution)/shard_map/ppermute | solution.py:21
  41.5 9.7 %collective-permute-start.4 = (bf16[64,256]{1,0:T(8,128)(2,1)S(1)}, bf16[64,256]{1,0:T(8,128)(2,1)S(1)}, u32[]{:S(2)}, u32[]{:S(2)}) collective-permute-start(bf16[64,256]{1,0:T(8,128)(2,1)S(1)} %get-tuple-element.89), channel_id=1, source_target_pairs={{0,20},{4,16},{8,28},{12,24},{16,4},{20,0},{24,12},{28,8},{1,21},{... | collective-permute-start | bytes 98312 | tf_op jit(solution)/shard_map/ppermute | solution.py:21
  44.4 7.6 %collective-permute-start.5 = (bf16[64,256]{1,0:T(8,128)(2,1)S(1)}, bf16[64,256]{1,0:T(8,128)(2,1)S(1)}, u32[]{:S(2)}, u32[]{:S(2)}) collective-permute-start(bf16[64,256]{1,0:T(8,128)(2,1)S(1)} %get-tuple-element.95), channel_id=1, source_target_pairs={{0,24},{4,28},{8,16},{12,20},{16,8},{20,12},{24,0},{28,4},{1,25},{... | collective-permute-start | bytes 98312 | tf_op jit(solution)/shard_map/ppermute | solution.py:21
  45.8 6.6 %collective-permute-start.6 = (bf16[64,256]{1,0:T(8,128)(2,1)S(1)}, bf16[64,256]{1,0:T(8,128)(2,1)S(1)}, u32[]{:S(2)}, u32[]{:S(2)}) collective-permute-start(bf16[64,256]{1,0:T(8,128)(2,1)S(1)} %get-tuple-element.88), channel_id=1, source_target_pairs={{0,28},{4,24},{8,20},{12,16},{16,12},{20,8},{24,4},{28,0},{1,29},{... | collective-permute-start | bytes 98312 | tf_op jit(solution)/shard_map/ppermute | solution.py:21
Sparse Core Ops, SparseCore 0:
  23.8 15.6 all-gather.2
  41.1 16.6 all-gather.4
